TPU v7x, 32 devices: a whole 2x2x4 slice. The times are simulated.
32 devices in a mesh: gx: 8 (over z, core), gy: 4 (over y, x).
Axes of the slice: x: 2, y: 2, z: 4, core: 2. Of those that a mesh axis runs over, the one named last changes fastest.
Arguments:
- raw_stack: float32 [2, 32, 128, 2048], P(None, ('gx', 'gy')), may hold values from 0 to 8
- psf_taps: float32 [3, 2, 31], replicated, may hold values from 0.05 to 1
Outputs:
- estimate: float32 [2, 32, 128, 2048], P(None, None, 'gy', 'gx')
All inputs are finite; a program needn't handle non-finite values.
Results may differ from a plain program's by a relative error of at most 0.0001.
Values sent between devices are 32-bit elements; how exact they have to be, the bound alone decides.
A program may use at most 192 MiB of HBM per device.

v0:
```python
import functools

import jax
import jax.numpy as jnp
from jax import lax
from jax.experimental import pallas as pl
from jax.experimental.pallas import tpu as pltpu
from jax.sharding import PartitionSpec as P

ITERS = 2
BACKGROUND = 0.5
SIGMA_ACROSS = 48.0
SIGMA_ALONG = 96.0
SUB = 8
CHUNKS = 4
MESH = pl.DeviceIdType.MESH


def smoothing_table(length_cells, spread_cells):
    rows = lax.broadcasted_iota(jnp.int32, (length_cells, length_cells), 0)
    columns = lax.broadcasted_iota(jnp.int32, (length_cells, length_cells), 1)
    scaled = (rows - columns).astype(jnp.float32) / spread_cells
    kernel_table = jnp.exp(-0.5 * scaled * scaled)
    return kernel_table / jnp.sum(kernel_table, axis=1, keepdims=True)


def circular_row(length_cells, spread_cells):
    places = lax.broadcasted_iota(jnp.int32, (1, length_cells), 1)
    scaled = jnp.minimum(places, length_cells - places).astype(jnp.float32) / spread_cells
    kernel_row = jnp.exp(-0.5 * scaled * scaled)
    return kernel_row / jnp.sum(kernel_row, axis=1, keepdims=True)


def base_rows(taps, axis, channel, reach, lag_of):
    count = taps.shape[2]
    width = -(-2 * reach // 128) * 128
    place = lax.broadcasted_iota(jnp.int32, (1, width), 1)
    lag = lag_of(jnp.where(place < width // 2, place, place - width))
    forward = jnp.zeros((1, width), jnp.float32)
    backward = forward
    total = forward
    for k in range(count):
        tap = taps[axis, channel, k]
        total = total + tap
        forward = jnp.where(lag == k, tap, forward)
        backward = jnp.where(lag == count - 1 - k, tap, backward)
    return forward / total, backward / total


def shifted(base, start, count, columns):
    block = jnp.broadcast_to(base, (count, base.shape[1]))
    block = pltpu.roll(block, start, 1, stride=1, stride_axis=0)[:, :columns]
    high = block.astype(jnp.bfloat16)
    return high, (block - high.astype(jnp.float32)).astype(jnp.bfloat16)


def fill_tables(taps, channel, edge, cells, depth, rows, middle, ends):
    size, width = depth.shape[2], rows.shape[1] // 2
    half = taps.shape[2] // 2
    depth_base = base_rows(
        taps, 0, channel, size,
        lambda d: jnp.where((d & (SUB - 1)) == 0, (d >> (SUB.bit_length() - 1)) + half, -1),
    )
    rows_base = base_rows(taps, 1, channel, width, lambda d: half - d)
    lines_base = base_rows(taps, 2, channel, max(cells, 3 * edge), lambda d: d - edge + half)
    for way in range(2):
        for start in range(0, size, 256):
            high, low = shifted(depth_base[way], start, min(256, size), size)
            depth[way, pl.ds(start, high.shape[0])] = high
            depth[way, pl.ds(size + start, high.shape[0])] = low
        high, low = shifted(rows_base[way], 0, width, width)
        both = jnp.concatenate([high, low], axis=1)
        rows[way] = jnp.concatenate([both, both], axis=0)
        if cells > 2 * edge:
            high, low = shifted(lines_base[way], 0, cells - 2 * edge, cells)
            middle[way] = jnp.concatenate([high, low], axis=0)
        high, low = shifted(lines_base[way], 0, edge, 3 * edge)
        ends[way] = jnp.concatenate([high, low], axis=0)


def split(value):
    high = value.astype(jnp.bfloat16)
    low = (value - high.astype(jnp.float32)).astype(jnp.bfloat16)
    return jnp.concatenate([high, low], axis=1)


def place_of(count_gy, pair, gy):
    first = gy // 2
    along = 2 * first + (gy % 2 + first) % 2
    odd = pair % 2
    return (1 - odd) * along + odd * (count_gy - 1 - along)


def device_of(count_gy, line):
    pair, place = line // count_gy, line % count_gy
    odd = pair % 2
    along = (1 - odd) * place + odd * (count_gy - 1 - place)
    first = along // 2
    return pair, 2 * first + (along % 2 + first) % 2


def deconvolve_kernel(
    count_gx, count_gy, edge, raw, taps, out,
    cleaned, estimate, ratio, wide, stage, along, smooth, across, depth, rows, middle, ends,
    held, send_sem, recv_sem, out_send, out_recv, own_sem, plane_send, plane_recv, held_sem,
):
    planes, cells, width = cleaned.shape
    size = planes * SUB
    gx, gy = lax.axis_index("gx"), lax.axis_index("gy")
    pair, core = gx // 2, gx % 2
    place = place_of(count_gy, pair, gy)
    line = pair * count_gy + place
    last = count_gx // 2 * count_gy - 1
    per_gx = count_gy // 2
    lines_x = width // count_gy
    me = gx * count_gy + gy

    def load(channel):
        return pltpu.make_async_copy(raw.at[channel, 0], held, held_sem)

    load(0).start()
    barrier = pltpu.get_barrier_semaphore()

    @pl.loop(0, count_gx * count_gy)
    def _(other):
        @pl.when(other != me)
        def _():
            pl.semaphore_signal(
                barrier, inc=1, device_id=(other // count_gy, other % count_gy), device_id_type=MESH
            )

    channels, _, _, lines_y = raw.shape
    block = along.shape[0] // 2
    blocks = lines_y // block
    chunks = lines_y // cells
    per_block = block // cells
    table = smoothing_table(width, SIGMA_ACROSS)
    high = table.astype(jnp.bfloat16)
    across[0:width] = high
    across[width : 2 * width] = (table - high.astype(jnp.float32)).astype(jnp.bfloat16)
    high, low = shifted(circular_row(lines_y, SIGMA_ALONG), 0, block, lines_y)
    along[0:block] = high
    along[block : 2 * block] = low

    def smooth_block(index):
        columns = pl.ds(pl.multiple_of(index * block, block), block)
        value = held[:, columns]
        high = value.astype(jnp.bfloat16)
        low = (value - high.astype(jnp.float32)).astype(jnp.bfloat16)
        product = jnp.dot(across[...], high, preferred_element_type=jnp.float32)
        total = product[:width] + product[width:]
        total += jnp.dot(across[0:width], low, preferred_element_type=jnp.float32)
        high = total.astype(jnp.bfloat16)
        smooth[0:width, columns] = high
        smooth[width : 2 * width, columns] = (total - high.astype(jnp.float32)).astype(jnp.bfloat16)

    def clean_block(channel, index):
        total = jnp.zeros((width, block), jnp.float32)
        for other in range(blocks):
            columns = pl.ds(other * block, block)
            shift = lax.rem(index - other + blocks, blocks)
            table = pl.ds(pl.multiple_of(shift * block, block), block)
            product = jnp.dot(
                smooth[:, columns], along[0:block, table], preferred_element_type=jnp.float32
            )
            total += product[:width] + product[width:]
            total += jnp.dot(
                smooth[0:width, columns], along[block : 2 * block, table],
                preferred_element_type=jnp.float32,
            )
        columns = pl.ds(pl.multiple_of(index * block, block), block)
        smoothed = smooth[0:width, columns].astype(jnp.float32)
        smoothed += smooth[width : 2 * width, columns].astype(jnp.float32)
        value = jnp.maximum(held[:, columns] - (smoothed - total), 0.0)
        estimate[pl.ds(channel * chunks + index * per_block, per_block)] = value.T.reshape(
            per_block, cells, width
        )

    def plane_copy(channel, chunk):
        target_pair, target_gy = device_of(count_gy, chunk)
        return pltpu.make_async_remote_copy(
            src_ref=estimate.at[channel * chunks + chunk],
            dst_ref=cleaned.at[me],
            send_sem=plane_send.at[channel * chunks + chunk],
            recv_sem=plane_recv.at[me],
            device_id=(target_pair * 2 + channel, target_gy),
            device_id_type=MESH,
        )

    own_plane = pltpu.make_async_copy(
        estimate.at[core * chunks + line], cleaned.at[me], plane_send.at[core * chunks + line]
    )

    def is_own_plane(channel, chunk):
        return jnp.logical_and(channel == core, chunk == line)

    for channel in range(channels):
        if channel > 0:
            load(channel).start()
        load(channel).wait()

        @pl.loop(0, blocks, unroll=2)
        def _(index):
            smooth_block(index)

        if channel == 0:
            pl.semaphore_wait(barrier, count_gx * count_gy - 1)

        @pl.loop(0, blocks)
        def _(step):
            index = lax.rem(step + (line + 1) // per_block + blocks // 2, blocks)
            clean_block(channel, index)
            for part in range(per_block):
                chunk = index * per_block + part

                @pl.when(is_own_plane(channel, chunk))
                def _():
                    own_plane.start()

                @pl.when(jnp.logical_not(is_own_plane(channel, chunk)))
                def _():
                    plane_copy(channel, chunk).start()

    fill_tables(taps, core, edge, cells, depth, rows, middle, ends)

    zeros = jnp.zeros((planes, edge, width), jnp.float32)

    @pl.when(line == 0)
    def _():
        for slot in range(2):
            wide[slot, :, 0:edge, :] = zeros

    @pl.when(line == last)
    def _():
        for slot in range(2):
            wide[slot, :, edge + cells :, :] = zeros

    own_plane.wait()
    for channel in range(channels):

        @pl.loop(0, chunks)
        def _(chunk):
            @pl.when(jnp.logical_not(is_own_plane(channel, chunk)))
            def _():
                plane_copy(channel, chunk).wait_send()

    @pl.loop(0, count_gx * count_gy)
    def _(other):
        @pl.when(other != me)
        def _():
            pltpu.make_async_remote_copy(
                src_ref=estimate.at[0],
                dst_ref=cleaned.at[other],
                send_sem=plane_send.at[0],
                recv_sem=plane_recv.at[other],
                device_id=(gx, gy),
                device_id_type=MESH,
            ).wait_recv()

    def edge_copy(slot, up):
        target_pair, target_gy = device_of(count_gy, line + (1 if up else -1))
        source = cells if up else edge
        target = 0 if up else edge + cells
        side = 1 if up else 0
        return pltpu.make_async_remote_copy(
            src_ref=wide.at[slot, :, pl.ds(source, edge), :],
            dst_ref=wide.at[slot, :, pl.ds(target, edge), :],
            send_sem=send_sem.at[slot, side],
            recv_sem=recv_sem.at[slot, side],
            device_id=(target_pair * 2 + core, target_gy),
            device_id_type=MESH,
        )

    def planes_and_rows(field, slot, way, group):
        start = pl.multiple_of(group * SUB, SUB)
        value = field[:, pl.ds(start, SUB), :].reshape(size, width)
        value = jnp.dot(depth[way], split(value), preferred_element_type=jnp.float32)
        value = value[:size] + value[size:]
        value = value[:, :width] + value[:, width:]
        value = jnp.dot(split(value), rows[way], preferred_element_type=jnp.float32)
        value = value[:, :width] + value[:, width:]
        wide[slot, :, pl.ds(edge + start, SUB), :] = value.reshape(planes, SUB, width)

    inner = cells - 2 * edge

    def along_middle(slot, way, plane):
        value = split(wide[slot, plane, edge : edge + cells])
        value = jnp.dot(middle[way], value, preferred_element_type=jnp.float32)
        value = value[:inner] + value[inner:]
        return value[:, :width] + value[:, width:]

    def along_ends(slot, way, plane):
        low = wide[slot, plane, 0 : 3 * edge]
        high = wide[slot, plane, cells - edge : cells + 2 * edge]
        value = split(jnp.concatenate([low, high], axis=1))
        value = jnp.dot(ends[way], value, preferred_element_type=jnp.float32)
        value = value[:edge] + value[edge:]
        value = value[:, : 2 * width] + value[:, 2 * width :]
        return value[:, :width], value[:, width:]

    unroll = 8 if size <= 256 else 1
    groups = cells // SUB
    outer = edge // SUB

    def filter_ends(field, slot, way):
        @pl.loop(0, 2 * outer, unroll=4 if size <= 256 else 1)
        def _(step):
            planes_and_rows(field, slot, way, lax.rem(step + groups - outer, groups))

        @pl.when(line > 0)
        def _():
            edge_copy(slot, False).start()

        @pl.when(line < last)
        def _():
            edge_copy(slot, True).start()

    def filter_middle(field, slot, way):
        if inner:

            @pl.loop(outer, groups - outer, unroll=4 if size <= 256 and groups % 4 == 0 else 1)
            def _(group):
                planes_and_rows(field, slot, way, group)

    def wait_ends(slot):
        @pl.when(line > 0)
        def _():
            edge_copy(slot, False).wait_send()
            edge_copy(slot, True).wait_recv()

        @pl.when(line < last)
        def _():
            edge_copy(slot, True).wait_send()
            edge_copy(slot, False).wait_recv()

    def out_copy(chunk, target_gy):
        part = pl.ds(chunk * (planes // CHUNKS), planes // CHUNKS)
        return pltpu.make_async_remote_copy(
            src_ref=stage.at[target_gy, part],
            dst_ref=out.at[core, place % per_gx, part],
            send_sem=out_send.at[chunk, target_gy],
            recv_sem=out_recv.at[chunk, core, place % per_gx],
            device_id=(pair * 2 + place // per_gx, target_gy),
            device_id_type=MESH,
        )

    def own_copy(chunk):
        part = pl.ds(chunk * (planes // CHUNKS), planes // CHUNKS)
        return pltpu.make_async_copy(
            stage.at[gy, part], out.at[core, place % per_gx, part], own_sem.at[chunk]
        )

    def is_own(target_gy):
        return jnp.logical_and(target_gy == gy, place // per_gx == core)

    low_end = slice(0, edge)
    high_end = slice(cells - edge, cells)
    between = slice(edge, cells - edge)
    filter_ends(cleaned, 0, 0)
    for iteration in range(ITERS):
        source = cleaned if iteration == 0 else estimate
        filter_middle(source, 0, 0)
        if inner:

            @pl.loop(0, planes, unroll=unroll)
            def _(plane):
                blurred = along_middle(0, 0, plane) + BACKGROUND
                ratio[plane, between] = cleaned[plane, between] / blurred

        wait_ends(0)

        @pl.loop(0, planes, unroll=unroll)
        def _(plane):
            low, high = along_ends(0, 0, plane)
            ratio[plane, low_end] = cleaned[plane, low_end] / (low + BACKGROUND)
            ratio[plane, high_end] = cleaned[plane, high_end] / (high + BACKGROUND)

        filter_ends(ratio, 1, 1)
        filter_middle(ratio, 1, 1)
        if inner:

            @pl.loop(0, planes, unroll=unroll)
            def _(plane):
                estimate[plane, between] = source[plane, between] * along_middle(1, 1, plane)

        wait_ends(1)
        if iteration < ITERS - 1:

            @pl.loop(0, planes, unroll=unroll)
            def _(plane):
                low, high = along_ends(1, 1, plane)
                estimate[plane, low_end] = source[plane, low_end] * low
                estimate[plane, high_end] = source[plane, high_end] * high

            filter_ends(estimate, 0, 0)
        else:
            for chunk in range(CHUNKS):

                @pl.loop(chunk * (planes // CHUNKS), (chunk + 1) * (planes // CHUNKS), unroll=unroll)
                def _(plane):
                    low, high = along_ends(1, 1, plane)
                    pieces = [source[plane, low_end] * low]
                    if inner:
                        pieces.append(estimate[plane, between])
                    pieces.append(source[plane, high_end] * high)
                    value = jnp.concatenate(pieces, axis=0).T
                    for target in range(count_gy):
                        stage[target, plane] = value[target * lines_x : (target + 1) * lines_x]

                for step in range(count_gy):
                    target = lax.rem(gy + 1 + step, count_gy)

                    @pl.when(is_own(target))
                    def _():
                        own_copy(chunk).start()

                    @pl.when(jnp.logical_not(is_own(target)))
                    def _():
                        out_copy(chunk, target).start()

    for chunk in range(CHUNKS):
        part = pl.ds(chunk * (planes // CHUNKS), planes // CHUNKS)
        for target in range(count_gy):

            @pl.when(is_own(target))
            def _():
                own_copy(chunk).wait()

            @pl.when(jnp.logical_not(is_own(target)))
            def _():
                out_copy(chunk, target).wait_send()

        for channel in range(2):
            for slot in range(per_gx):
                mine = jnp.logical_and(channel == core, place == core * per_gx + slot)

                @pl.when(jnp.logical_not(mine))
                def _():
                    pltpu.make_async_remote_copy(
                        src_ref=stage.at[0, part],
                        dst_ref=out.at[channel, slot, part],
                        send_sem=out_send.at[chunk, 0],
                        recv_sem=out_recv.at[chunk, channel, slot],
                        device_id=(gx, gy),
                        device_id_type=MESH,
                    ).wait_recv()


def local(raw_stack, psf_taps):
    channels, own_planes, lines_x, lines_y = raw_stack.shape
    half_taps = psf_taps.shape[2] // 2
    count_gx = lax.axis_size("gx")
    count_gy = lax.axis_size("gy")
    pairs = count_gx // channels
    cells = lines_y // (pairs * count_gy)
    planes = own_planes * count_gx * count_gy
    edge = -(-half_taps // SUB) * SUB

    block = min(lines_y, 256)
    size = planes * SUB
    per_gx = count_gy // 2
    block_x = lines_x // count_gy
    field = pltpu.VMEM((planes, cells, lines_x), jnp.float32)
    gathered = pl.pallas_call(
        functools.partial(deconvolve_kernel, count_gx, count_gy, edge),
        out_shape=jax.ShapeDtypeStruct((channels, per_gx, planes, block_x, cells), jnp.float32),
        in_specs=[pl.BlockSpec(memory_space=pl.ANY), pl.BlockSpec(memory_space=pltpu.SMEM)],
        out_specs=pl.BlockSpec(memory_space=pl.ANY),
        scratch_shapes=[
            field,
            field,
            field,
            pltpu.VMEM((2, planes, cells + 2 * edge, lines_x), jnp.float32),
            pltpu.VMEM((count_gy, planes, block_x, cells), jnp.float32),
            pltpu.VMEM((2 * block, lines_y), jnp.bfloat16),
            pltpu.VMEM((2 * lines_x, lines_y), jnp.bfloat16),
            pltpu.VMEM((2 * lines_x, lines_x), jnp.bfloat16),
            pltpu.VMEM((2, 2 * size, size), jnp.bfloat16),
            pltpu.VMEM((2, 2 * lines_x, 2 * lines_x), jnp.bfloat16),
            pltpu.VMEM((2, 2 * max(cells - 2 * edge, edge), cells), jnp.bfloat16),
            pltpu.VMEM((2, 2 * edge, 3 * edge), jnp.bfloat16),
            pltpu.VMEM((lines_x, lines_y), jnp.float32),
            pltpu.SemaphoreType.DMA((2, 2)),
            pltpu.SemaphoreType.DMA((2, 2)),
            pltpu.SemaphoreType.DMA((CHUNKS, count_gy)),
            pltpu.SemaphoreType.DMA((CHUNKS, channels, per_gx)),
            pltpu.SemaphoreType.DMA((CHUNKS,)),
            pltpu.SemaphoreType.DMA((planes,)),
            pltpu.SemaphoreType.DMA((planes,)),
            pltpu.SemaphoreType.DMA,
        ],
        compiler_params=pltpu.CompilerParams(
            collective_id=0, has_side_effects=True, vmem_limit_bytes=67043328
        ),
    )(raw_stack, psf_taps)
    return jnp.transpose(gathered, (0, 2, 3, 1, 4)).reshape(
        channels, planes, block_x, per_gx * cells
    )


def solution(mesh):
    in_specs = (P(None, ("gx", "gy"), None, None), P())
    out_specs = P(None, None, "gy", "gx")
    return jax.shard_map(local, mesh=mesh, in_specs=in_specs, out_specs=out_specs, check_vma=False)
```

profile of v0, /device:TPU:1, one launch (start us, length us, event | category | flops | bytes accessed | tf_op | source)
XLA Modules:
  0.0 117.2 jit_solution(17478814978637800478)
XLA Ops:
  0.0 114.0 %shard_map.28 = f32[2,2,32,32,128]{4,3,2,1,0:T(8,128)} custom-call(f32[2,1,128,2048]{3,2,1,0:T(8,128)} %raw.1, f32[3,2,31]{2,1,0:T(2,128)} %taps.1), custom_call_target="tpu_custom_call" | custom-call | tf_op jit(solution)/shard_map/pallas_call | solution.py:464
  114.1 3.1 %copy_bitcast_fusion = f32[2,32,32,256]{3,2,1,0:T(8,128)} fusion(f32[2,2,32,32,128]{4,3,2,1,0:T(8,128)} %shard_map.28), kind=kLoop, calls=%fused_computation | loop fusion | bytes 4194304 | tf_op jit(solution)/shard_map/reshape | solution.py:496
where the time goes:
time: 118 us; the launch traced here: 117 us
  Pallas kernels  114 us (97%)
  local copies, waits for them, and re-layouts  3.1 us (3%)
    pallas_call x1, Pallas kernels, local(): pl.pallas_call(functools.partial(deconvolve_kernel, count_gx, count_gy, e...  114 us
    reshape x1, local copies, waits for them, and re-layouts, local(): jnp.transpose(gathered, (0, 2, 3, 1, 4))  3.1 us

commit v1 on v0

--- a/solution.py
+++ b/solution.py
@@ -55,33 +55,36 @@
 
 
 def fill_tables(taps, channel, edge, cells, depth, rows, middle, ends):
-    size, width = depth.shape[2], rows.shape[1] // 2
+    planes, width = depth.shape[1], rows.shape[1] // 2
     half = taps.shape[2] // 2
-    depth_base = base_rows(
-        taps, 0, channel, size,
-        lambda d: jnp.where((d & (SUB - 1)) == 0, (d >> (SUB.bit_length() - 1)) + half, -1),
-    )
+    depth_base = base_rows(taps, 0, channel, planes, lambda d: d + half)
     rows_base = base_rows(taps, 1, channel, width, lambda d: half - d)
     lines_base = base_rows(taps, 2, channel, max(cells, 3 * edge), lambda d: d - edge + half)
     for way in range(2):
-        for start in range(0, size, 256):
-            high, low = shifted(depth_base[way], start, min(256, size), size)
-            depth[way, pl.ds(start, high.shape[0])] = high
-            depth[way, pl.ds(size + start, high.shape[0])] = low
+        high, low = shifted(depth_base[way], 0, planes, planes)
+        depth[way] = jnp.concatenate([high, high, low], axis=1)
         high, low = shifted(rows_base[way], 0, width, width)
         both = jnp.concatenate([high, low], axis=1)
         rows[way] = jnp.concatenate([both, both], axis=0)
         if cells > 2 * edge:
             high, low = shifted(lines_base[way], 0, cells - 2 * edge, cells)
-            middle[way] = jnp.concatenate([high, low], axis=0)
+            middle[way] = twice(high, low)
         high, low = shifted(lines_base[way], 0, edge, 3 * edge)
-        ends[way] = jnp.concatenate([high, low], axis=0)
-
-
-def split(value):
+        ends[way] = twice(high, low)
+
+
+def twice(high, low):
+    both = jnp.concatenate([high, low], axis=0)
+    return jnp.concatenate([both, both], axis=1)
+
+
+def halves(value):
     high = value.astype(jnp.bfloat16)
-    low = (value - high.astype(jnp.float32)).astype(jnp.bfloat16)
-    return jnp.concatenate([high, low], axis=1)
+    return high, (value - high.astype(jnp.float32)).astype(jnp.bfloat16)
+
+
+def split(value, axis):
+    return jnp.concatenate(halves(value), axis=axis)
 
 
 def place_of(count_gy, pair, gy):
@@ -101,11 +104,13 @@
 
 def deconvolve_kernel(
     count_gx, count_gy, edge, raw, taps, out,
-    cleaned, estimate, ratio, wide, stage, along, smooth, across, depth, rows, middle, ends,
+    cleaned, estimate, ratio, wide0, wide1, leaving, stage, along, smooth, across, depth, rows, middle, ends,
     held, send_sem, recv_sem, out_send, out_recv, own_sem, plane_send, plane_recv, held_sem,
 ):
-    planes, cells, width = cleaned.shape
+    groups, planes, _, width = cleaned.shape
+    cells = groups * SUB
     size = planes * SUB
+    wide = (wide0, wide1)
     gx, gy = lax.axis_index("gx"), lax.axis_index("gy")
     pair, core = gx // 2, gx % 2
     place = place_of(count_gy, pair, gy)
@@ -172,15 +177,15 @@
         smoothed = smooth[0:width, columns].astype(jnp.float32)
         smoothed += smooth[width : 2 * width, columns].astype(jnp.float32)
         value = jnp.maximum(held[:, columns] - (smoothed - total), 0.0)
-        estimate[pl.ds(channel * chunks + index * per_block, per_block)] = value.T.reshape(
-            per_block, cells, width
+        leaving[pl.ds(channel * chunks + index * per_block, per_block)] = value.T.reshape(
+            per_block, groups, SUB, width
         )
 
     def plane_copy(channel, chunk):
         target_pair, target_gy = device_of(count_gy, chunk)
         return pltpu.make_async_remote_copy(
-            src_ref=estimate.at[channel * chunks + chunk],
-            dst_ref=cleaned.at[me],
+            src_ref=leaving.at[channel * chunks + chunk],
+            dst_ref=cleaned.at[:, me],
             send_sem=plane_send.at[channel * chunks + chunk],
             recv_sem=plane_recv.at[me],
             device_id=(target_pair * 2 + channel, target_gy),
@@ -188,7 +193,7 @@
         )
 
     own_plane = pltpu.make_async_copy(
-        estimate.at[core * chunks + line], cleaned.at[me], plane_send.at[core * chunks + line]
+        leaving.at[core * chunks + line], cleaned.at[:, me], plane_send.at[core * chunks + line]
     )
 
     def is_own_plane(channel, chunk):
@@ -223,17 +228,18 @@
 
     fill_tables(taps, core, edge, cells, depth, rows, middle, ends)
 
-    zeros = jnp.zeros((planes, edge, width), jnp.float32)
+    outer = edge // SUB
+    zeros = jnp.zeros((outer, planes, SUB, width), jnp.float32)
 
     @pl.when(line == 0)
     def _():
         for slot in range(2):
-            wide[slot, :, 0:edge, :] = zeros
+            wide[slot][0:outer] = zeros
 
     @pl.when(line == last)
     def _():
         for slot in range(2):
-            wide[slot, :, edge + cells :, :] = zeros
+            wide[slot][outer + groups :] = zeros
 
     own_plane.wait()
     for channel in range(channels):
@@ -249,8 +255,8 @@
         @pl.when(other != me)
         def _():
             pltpu.make_async_remote_copy(
-                src_ref=estimate.at[0],
-                dst_ref=cleaned.at[other],
+                src_ref=leaving.at[0],
+                dst_ref=cleaned.at[:, other],
                 send_sem=plane_send.at[0],
                 recv_sem=plane_recv.at[other],
                 device_id=(gx, gy),
@@ -259,53 +265,81 @@
 
     def edge_copy(slot, up):
         target_pair, target_gy = device_of(count_gy, line + (1 if up else -1))
-        source = cells if up else edge
-        target = 0 if up else edge + cells
+        source = groups if up else outer
+        target = 0 if up else outer + groups
         side = 1 if up else 0
         return pltpu.make_async_remote_copy(
-            src_ref=wide.at[slot, :, pl.ds(source, edge), :],
-            dst_ref=wide.at[slot, :, pl.ds(target, edge), :],
+            src_ref=wide[slot].at[pl.ds(source, outer)],
+            dst_ref=wide[slot].at[pl.ds(target, outer)],
             send_sem=send_sem.at[slot, side],
             recv_sem=recv_sem.at[slot, side],
             device_id=(target_pair * 2 + core, target_gy),
             device_id_type=MESH,
         )
 
-    def planes_and_rows(field, slot, way, group):
-        start = pl.multiple_of(group * SUB, SUB)
-        value = field[:, pl.ds(start, SUB), :].reshape(size, width)
-        value = jnp.dot(depth[way], split(value), preferred_element_type=jnp.float32)
-        value = value[:size] + value[size:]
+    def get_cell(ref, group, cell):
+        if width > 128:
+            return ref[group, :, cell, :]
+        start = pl.multiple_of(group * size, size)
+        return ref.reshape(ref.shape[0] * size, width)[pl.ds(start + cell, planes, stride=SUB), :]
+
+    def set_cell(ref, group, cell, value):
+        if width > 128:
+            ref[group, :, cell, :] = value
+        else:
+            start = pl.multiple_of(group * size, size)
+            ref.reshape(ref.shape[0] * size, width)[pl.ds(start + cell, planes, stride=SUB), :] = value
+
+    def planes_and_rows(field, slot, way, places):
+        pieces = []
+        for group in places:
+            for cell in range(0, SUB, 2):
+                value = [get_cell(field, group, cell + k) for k in range(2)]
+                high, low = halves(jnp.concatenate(value, axis=1))
+                value = jnp.concatenate([high, low, high], axis=0)
+                value = jnp.dot(depth[way], value, preferred_element_type=jnp.float32)
+                pieces += [value[:, :width], value[:, width:]]
+        value = split(jnp.concatenate(pieces, axis=0), 1)
+        value = jnp.dot(value, rows[way], preferred_element_type=jnp.float32)
         value = value[:, :width] + value[:, width:]
-        value = jnp.dot(split(value), rows[way], preferred_element_type=jnp.float32)
-        value = value[:, :width] + value[:, width:]
-        wide[slot, :, pl.ds(edge + start, SUB), :] = value.reshape(planes, SUB, width)
+        for at, group in enumerate(places):
+            for cell in range(SUB):
+                first = (at * SUB + cell) * planes
+                set_cell(wide[slot], outer + group, cell, value[first : first + planes])
 
     inner = cells - 2 * edge
 
+    def lines(ref, plane, first, count):
+        return ref[pl.ds(first, count), plane].reshape(count * SUB, width)
+
+    def keep(ref, plane, first, value):
+        count = value.shape[0] // SUB
+        ref[pl.ds(first, count), plane] = value.reshape(count, SUB, width)
+
+    def along_table(table, count, value):
+        value = jnp.dot(table, split(value, 0), preferred_element_type=jnp.float32)
+        value = value[:count] + value[count:]
+        return value[:, :width], value[:, width:]
+
     def along_middle(slot, way, plane):
-        value = split(wide[slot, plane, edge : edge + cells])
-        value = jnp.dot(middle[way], value, preferred_element_type=jnp.float32)
-        value = value[:inner] + value[inner:]
-        return value[:, :width] + value[:, width:]
+        value = [lines(wide[slot], plane + k, outer, groups) for k in range(2)]
+        return along_table(middle[way], inner, jnp.concatenate(value, axis=1))
 
     def along_ends(slot, way, plane):
-        low = wide[slot, plane, 0 : 3 * edge]
-        high = wide[slot, plane, cells - edge : cells + 2 * edge]
-        value = split(jnp.concatenate([low, high], axis=1))
-        value = jnp.dot(ends[way], value, preferred_element_type=jnp.float32)
-        value = value[:edge] + value[edge:]
-        value = value[:, : 2 * width] + value[:, 2 * width :]
-        return value[:, :width], value[:, width:]
-
-    unroll = 8 if size <= 256 else 1
-    groups = cells // SUB
-    outer = edge // SUB
+        low = lines(wide[slot], plane, 0, 3 * outer)
+        high = lines(wide[slot], plane, groups - outer, 3 * outer)
+        return along_table(ends[way], edge, jnp.concatenate([low, high], axis=1))
+
+    small = size * width <= 65536
+    unroll = 8 if small else 1
+    batch = 4 if small else 1
+
+    def filter_places(field, slot, way, places):
+        for first in range(0, len(places), batch):
+            planes_and_rows(field, slot, way, places[first : first + batch])
 
     def filter_ends(field, slot, way):
-        @pl.loop(0, 2 * outer, unroll=4 if size <= 256 else 1)
-        def _(step):
-            planes_and_rows(field, slot, way, lax.rem(step + groups - outer, groups))
+        filter_places(field, slot, way, [*range(outer), *range(groups - outer, groups)])
 
         @pl.when(line > 0)
         def _():
@@ -316,11 +350,14 @@
             edge_copy(slot, True).start()
 
     def filter_middle(field, slot, way):
+        count = groups - 2 * outer
+        step = batch if count % batch == 0 else 1
         if inner:
 
-            @pl.loop(outer, groups - outer, unroll=4 if size <= 256 and groups % 4 == 0 else 1)
-            def _(group):
-                planes_and_rows(field, slot, way, group)
+            @pl.loop(0, count // step)
+            def _(turn):
+                first = outer + turn * step
+                planes_and_rows(field, slot, way, [first + k for k in range(step)])
 
     def wait_ends(slot):
         @pl.when(line > 0)
@@ -353,44 +390,48 @@
     def is_own(target_gy):
         return jnp.logical_and(target_gy == gy, place // per_gx == core)
 
-    low_end = slice(0, edge)
-    high_end = slice(cells - edge, cells)
-    between = slice(edge, cells - edge)
+    top = groups - outer
+
+    def middle_lines(slot, way, use):
+        if inner:
+
+            @pl.loop(0, planes // 2, unroll=max(unroll // 2, 1))
+            def _(turn):
+                for k, value in enumerate(along_middle(slot, way, 2 * turn)):
+                    use(2 * turn + k, value)
+
+    def to_ratio(plane, first, value):
+        known = lines(cleaned, plane, first, value.shape[0] // SUB)
+        keep(ratio, plane, first, known / (value + BACKGROUND))
+
     filter_ends(cleaned, 0, 0)
     for iteration in range(ITERS):
         source = cleaned if iteration == 0 else estimate
+
+        def to_estimate(plane, first, value):
+            keep(estimate, plane, first, lines(source, plane, first, value.shape[0] // SUB) * value)
+
         filter_middle(source, 0, 0)
-        if inner:
-
-            @pl.loop(0, planes, unroll=unroll)
-            def _(plane):
-                blurred = along_middle(0, 0, plane) + BACKGROUND
-                ratio[plane, between] = cleaned[plane, between] / blurred
-
+        middle_lines(0, 0, lambda plane, value: to_ratio(plane, outer, value))
         wait_ends(0)
 
         @pl.loop(0, planes, unroll=unroll)
         def _(plane):
             low, high = along_ends(0, 0, plane)
-            ratio[plane, low_end] = cleaned[plane, low_end] / (low + BACKGROUND)
-            ratio[plane, high_end] = cleaned[plane, high_end] / (high + BACKGROUND)
+            to_ratio(plane, 0, low)
+            to_ratio(plane, top, high)
 
         filter_ends(ratio, 1, 1)
         filter_middle(ratio, 1, 1)
-        if inner:
-
-            @pl.loop(0, planes, unroll=unroll)
-            def _(plane):
-                estimate[plane, between] = source[plane, between] * along_middle(1, 1, plane)
-
+        middle_lines(1, 1, lambda plane, value: to_estimate(plane, outer, value))
         wait_ends(1)
         if iteration < ITERS - 1:
 
             @pl.loop(0, planes, unroll=unroll)
             def _(plane):
                 low, high = along_ends(1, 1, plane)
-                estimate[plane, low_end] = source[plane, low_end] * low
-                estimate[plane, high_end] = source[plane, high_end] * high
+                to_estimate(plane, 0, low)
+                to_estimate(plane, top, high)
 
             filter_ends(estimate, 0, 0)
         else:
@@ -399,10 +440,10 @@
                 @pl.loop(chunk * (planes // CHUNKS), (chunk + 1) * (planes // CHUNKS), unroll=unroll)
                 def _(plane):
                     low, high = along_ends(1, 1, plane)
-                    pieces = [source[plane, low_end] * low]
+                    pieces = [lines(source, plane, 0, outer) * low]
                     if inner:
-                        pieces.append(estimate[plane, between])
-                    pieces.append(source[plane, high_end] * high)
+                        pieces.append(lines(estimate, plane, outer, groups - 2 * outer))
+                    pieces.append(lines(source, plane, top, outer) * high)
                     value = jnp.concatenate(pieces, axis=0).T
                     for target in range(count_gy):
                         stage[target, plane] = value[target * lines_x : (target + 1) * lines_x]
@@ -457,10 +498,12 @@
     edge = -(-half_taps // SUB) * SUB
 
     block = min(lines_y, 256)
-    size = planes * SUB
+    groups = cells // SUB
+    outer = edge // SUB
     per_gx = count_gy // 2
     block_x = lines_x // count_gy
-    field = pltpu.VMEM((planes, cells, lines_x), jnp.float32)
+    field = pltpu.VMEM((groups, planes, SUB, lines_x), jnp.float32)
+    wide = pltpu.VMEM((groups + 2 * outer, planes, SUB, lines_x), jnp.float32)
     gathered = pl.pallas_call(
         functools.partial(deconvolve_kernel, count_gx, count_gy, edge),
         out_shape=jax.ShapeDtypeStruct((channels, per_gx, planes, block_x, cells), jnp.float32),
@@ -470,15 +513,17 @@
             field,
             field,
             field,
-            pltpu.VMEM((2, planes, cells + 2 * edge, lines_x), jnp.float32),
+            wide,
+            wide,
+            pltpu.VMEM((planes, groups, SUB, lines_x), jnp.float32),
             pltpu.VMEM((count_gy, planes, block_x, cells), jnp.float32),
             pltpu.VMEM((2 * block, lines_y), jnp.bfloat16),
             pltpu.VMEM((2 * lines_x, lines_y), jnp.bfloat16),
             pltpu.VMEM((2 * lines_x, lines_x), jnp.bfloat16),
-            pltpu.VMEM((2, 2 * size, size), jnp.bfloat16),
+            pltpu.VMEM((2, planes, 3 * planes), jnp.bfloat16),
             pltpu.VMEM((2, 2 * lines_x, 2 * lines_x), jnp.bfloat16),
-            pltpu.VMEM((2, 2 * max(cells - 2 * edge, edge), cells), jnp.bfloat16),
-            pltpu.VMEM((2, 2 * edge, 3 * edge), jnp.bfloat16),
+            pltpu.VMEM((2, 2 * max(cells - 2 * edge, edge), 2 * cells), jnp.bfloat16),
+            pltpu.VMEM((2, 2 * edge, 6 * edge), jnp.bfloat16),
             pltpu.VMEM((lines_x, lines_y), jnp.float32),
             pltpu.SemaphoreType.DMA((2, 2)),
             pltpu.SemaphoreType.DMA((2, 2)),

time: 118 us -> 114 us (0.966)
  Pallas kernels: 114 us -> 110 us
    pallas_call x1, Pallas kernels: 114 us -> 110 us  [local(): pl.pallas_call(functools.partial(deconvolve_kernel, count_gx, count_gy, e...]
where the time goes in v1:
time: 114 us
  Pallas kernels  110 us (96%)
  local copies, waits for them, and re-layouts  3.1 us (3%)
    pallas_call x1, Pallas kernels, local(): pl.pallas_call(functools.partial(deconvolve_kernel, count_gx, count_gy, e...  110 us
    reshape x1, local copies, waits for them, and re-layouts, local(): jnp.transpose(gathered, (0, 2, 3, 1, 4))  3.1 us

profile of v1, /device:TPU:1, one launch (start us, length us, event | category | flops | bytes accessed | tf_op | source)
XLA Modules:
  0.0 113.6 jit_solution(7094413604456612086)
XLA Ops:
  0.0 110.5 %shard_map.28 = f32[2,2,32,32,128]{4,3,2,1,0:T(8,128)} custom-call(f32[2,1,128,2048]{3,2,1,0:T(8,128)} %raw.1, f32[3,2,31]{2,1,0:T(2,128)} %taps.1), custom_call_target="tpu_custom_call" | custom-call | tf_op jit(solution)/shard_map/pallas_call | solution.py:507
  110.5 3.1 %copy_bitcast_fusion = f32[2,32,32,256]{3,2,1,0:T(8,128)} fusion(f32[2,2,32,32,128]{4,3,2,1,0:T(8,128)} %shard_map.28), kind=kLoop, calls=%fused_computation | loop fusion | bytes 4194304 | tf_op jit(solution)/shard_map/reshape | solution.py:541

commit v2 on v1

--- a/solution.py
+++ b/solution.py
@@ -87,19 +87,15 @@
     return jnp.concatenate(halves(value), axis=axis)
 
 
-def place_of(count_gy, pair, gy):
-    first = gy // 2
-    along = 2 * first + (gy % 2 + first) % 2
+def turned(count_gy, pair, along):
     odd = pair % 2
     return (1 - odd) * along + odd * (count_gy - 1 - along)
 
 
-def device_of(count_gy, line):
-    pair, place = line // count_gy, line % count_gy
-    odd = pair % 2
-    along = (1 - odd) * place + odd * (count_gy - 1 - place)
-    first = along // 2
-    return pair, 2 * first + (along % 2 + first) % 2
+def device_of(count_gy, channels, channel, line):
+    pair = line // count_gy
+    along = turned(count_gy, pair, line % count_gy)
+    return pair * 2 + along % 2, channel * (count_gy // channels) + along // 2
 
 
 def deconvolve_kernel(
@@ -113,7 +109,10 @@
     wide = (wide0, wide1)
     gx, gy = lax.axis_index("gx"), lax.axis_index("gy")
     pair, core = gx // 2, gx % 2
-    place = place_of(count_gy, pair, gy)
+    channels, _, _, lines_y = raw.shape
+    per_channel = count_gy // channels
+    mine = gy // per_channel
+    place = turned(count_gy, pair, gy % per_channel * 2 + core)
     line = pair * count_gy + place
     last = count_gx // 2 * count_gy - 1
     per_gx = count_gy // 2
@@ -123,7 +122,10 @@
     def load(channel):
         return pltpu.make_async_copy(raw.at[channel, 0], held, held_sem)
 
-    load(0).start()
+    def channel_of(turn):
+        return lax.rem(turn + core, channels)
+
+    load(channel_of(0)).start()
     barrier = pltpu.get_barrier_semaphore()
 
     @pl.loop(0, count_gx * count_gy)
@@ -134,7 +136,6 @@
                 barrier, inc=1, device_id=(other // count_gy, other % count_gy), device_id_type=MESH
             )
 
-    channels, _, _, lines_y = raw.shape
     block = along.shape[0] // 2
     blocks = lines_y // block
     chunks = lines_y // cells
@@ -182,25 +183,26 @@
         )
 
     def plane_copy(channel, chunk):
-        target_pair, target_gy = device_of(count_gy, chunk)
+        target_gx, target_gy = device_of(count_gy, channels, channel, chunk)
         return pltpu.make_async_remote_copy(
             src_ref=leaving.at[channel * chunks + chunk],
             dst_ref=cleaned.at[:, me],
             send_sem=plane_send.at[channel * chunks + chunk],
             recv_sem=plane_recv.at[me],
-            device_id=(target_pair * 2 + channel, target_gy),
+            device_id=(target_gx, target_gy),
             device_id_type=MESH,
         )
 
     own_plane = pltpu.make_async_copy(
-        leaving.at[core * chunks + line], cleaned.at[:, me], plane_send.at[core * chunks + line]
+        leaving.at[mine * chunks + line], cleaned.at[:, me], plane_send.at[mine * chunks + line]
     )
 
     def is_own_plane(channel, chunk):
-        return jnp.logical_and(channel == core, chunk == line)
-
-    for channel in range(channels):
-        if channel > 0:
+        return jnp.logical_and(channel == mine, chunk == line)
+
+    for turn in range(channels):
+        channel = channel_of(turn)
+        if turn > 0:
             load(channel).start()
         load(channel).wait()
 
@@ -208,7 +210,7 @@
         def _(index):
             smooth_block(index)
 
-        if channel == 0:
+        if turn == 0:
             pl.semaphore_wait(barrier, count_gx * count_gy - 1)
 
         @pl.loop(0, blocks)
@@ -226,7 +228,7 @@
                 def _():
                     plane_copy(channel, chunk).start()
 
-    fill_tables(taps, core, edge, cells, depth, rows, middle, ends)
+    fill_tables(taps, mine, edge, cells, depth, rows, middle, ends)
 
     outer = edge // SUB
     zeros = jnp.zeros((outer, planes, SUB, width), jnp.float32)
@@ -264,7 +266,7 @@
             ).wait_recv()
 
     def edge_copy(slot, up):
-        target_pair, target_gy = device_of(count_gy, line + (1 if up else -1))
+        target_gx, target_gy = device_of(count_gy, channels, mine, line + (1 if up else -1))
         source = groups if up else outer
         target = 0 if up else outer + groups
         side = 1 if up else 0
@@ -273,7 +275,7 @@
             dst_ref=wide[slot].at[pl.ds(target, outer)],
             send_sem=send_sem.at[slot, side],
             recv_sem=recv_sem.at[slot, side],
-            device_id=(target_pair * 2 + core, target_gy),
+            device_id=(target_gx, target_gy),
             device_id_type=MESH,
         )
 
@@ -374,9 +376,9 @@
         part = pl.ds(chunk * (planes // CHUNKS), planes // CHUNKS)
         return pltpu.make_async_remote_copy(
             src_ref=stage.at[target_gy, part],
-            dst_ref=out.at[core, place % per_gx, part],
+            dst_ref=out.at[mine, place % per_gx, part],
             send_sem=out_send.at[chunk, target_gy],
-            recv_sem=out_recv.at[chunk, core, place % per_gx],
+            recv_sem=out_recv.at[chunk, mine, place % per_gx],
             device_id=(pair * 2 + place // per_gx, target_gy),
             device_id_type=MESH,
         )
@@ -384,7 +386,7 @@
     def own_copy(chunk):
         part = pl.ds(chunk * (planes // CHUNKS), planes // CHUNKS)
         return pltpu.make_async_copy(
-            stage.at[gy, part], out.at[core, place % per_gx, part], own_sem.at[chunk]
+            stage.at[gy, part], out.at[mine, place % per_gx, part], own_sem.at[chunk]
         )
 
     def is_own(target_gy):
@@ -471,11 +473,11 @@
             def _():
                 out_copy(chunk, target).wait_send()
 
-        for channel in range(2):
+        for channel in range(channels):
             for slot in range(per_gx):
-                mine = jnp.logical_and(channel == core, place == core * per_gx + slot)
-
-                @pl.when(jnp.logical_not(mine))
+                here = jnp.logical_and(channel == mine, place == core * per_gx + slot)
+
+                @pl.when(jnp.logical_not(here))
                 def _():
                     pltpu.make_async_remote_copy(
                         src_ref=stage.at[0, part],
@@ -492,7 +494,7 @@
     half_taps = psf_taps.shape[2] // 2
     count_gx = lax.axis_size("gx")
     count_gy = lax.axis_size("gy")
-    pairs = count_gx // channels
+    pairs = count_gx // 2
     cells = lines_y // (pairs * count_gy)
     planes = own_planes * count_gx * count_gy
     edge = -(-half_taps // SUB) * SUB

time: 114 us -> 106 us (0.930)
  Pallas kernels: 110 us -> 102 us
    pallas_call x1, Pallas kernels: 110 us -> 102 us  [local(): pl.pallas_call(functools.partial(deconvolve_kernel, count_gx, count_gy, e...]
where the time goes in v2:
time: 106 us
  Pallas kernels  102 us (96%)
  local copies, waits for them, and re-layouts  3.1 us (3%)
    pallas_call x1, Pallas kernels, local(): pl.pallas_call(functools.partial(deconvolve_kernel, count_gx, count_gy, e...  102 us
    reshape x1, local copies, waits for them, and re-layouts, local(): jnp.transpose(gathered, (0, 2, 3, 1, 4))  3.1 us

profile of v2, /device:TPU:1, one launch (start us, length us, event | category | flops | bytes accessed | tf_op | source)
XLA Modules:
  0.0 105.6 jit_solution(12251636093835472356)
XLA Ops:
  0.0 102.5 %shard_map.28 = f32[2,2,32,32,128]{4,3,2,1,0:T(8,128)} custom-call(f32[2,1,128,2048]{3,2,1,0:T(8,128)} %raw.1, f32[3,2,31]{2,1,0:T(2,128)} %taps.1), custom_call_target="tpu_custom_call" | custom-call | tf_op jit(solution)/shard_map/pallas_call | solution.py:509
  102.5 3.1 %copy_bitcast_fusion = f32[2,32,32,256]{3,2,1,0:T(8,128)} fusion(f32[2,2,32,32,128]{4,3,2,1,0:T(8,128)} %shard_map.28), kind=kLoop, calls=%fused_computation | loop fusion | bytes 4194304 | tf_op jit(solution)/shard_map/reshape | solution.py:543

commit v3 on v2

--- a/solution.py
+++ b/solution.py
@@ -13,6 +13,7 @@
 SIGMA_ALONG = 96.0
 SUB = 8
 CHUNKS = 4
+PIECES = 4
 MESH = pl.DeviceIdType.MESH
 
 
@@ -265,16 +266,19 @@
                 device_id_type=MESH,
             ).wait_recv()
 
-    def edge_copy(slot, up):
+    per_piece = planes // PIECES
+
+    def edge_copy(slot, up, piece):
         target_gx, target_gy = device_of(count_gy, channels, mine, line + (1 if up else -1))
         source = groups if up else outer
         target = 0 if up else outer + groups
         side = 1 if up else 0
+        part = pl.ds(piece * per_piece, per_piece)
         return pltpu.make_async_remote_copy(
-            src_ref=wide[slot].at[pl.ds(source, outer)],
-            dst_ref=wide[slot].at[pl.ds(target, outer)],
-            send_sem=send_sem.at[slot, side],
-            recv_sem=recv_sem.at[slot, side],
+            src_ref=wide[slot].at[pl.ds(source, outer), part],
+            dst_ref=wide[slot].at[pl.ds(target, outer), part],
+            send_sem=send_sem.at[slot, side, piece],
+            recv_sem=recv_sem.at[slot, side, piece],
             device_id=(target_gx, target_gy),
             device_id_type=MESH,
         )
@@ -292,7 +296,7 @@
             start = pl.multiple_of(group * size, size)
             ref.reshape(ref.shape[0] * size, width)[pl.ds(start + cell, planes, stride=SUB), :] = value
 
-    def planes_and_rows(field, slot, way, places):
+    def planes_and_rows(field, way, places, put):
         pieces = []
         for group in places:
             for cell in range(0, SUB, 2):
@@ -307,7 +311,7 @@
         for at, group in enumerate(places):
             for cell in range(SUB):
                 first = (at * SUB + cell) * planes
-                set_cell(wide[slot], outer + group, cell, value[first : first + planes])
+                put(group, cell, value[first : first + planes])
 
     inner = cells - 2 * edge
 
@@ -336,41 +340,42 @@
     unroll = 8 if small else 1
     batch = 4 if small else 1
 
-    def filter_places(field, slot, way, places):
+    def filter_ends(field, way, put):
+        places = [*range(outer), *range(groups - outer, groups)]
         for first in range(0, len(places), batch):
-            planes_and_rows(field, slot, way, places[first : first + batch])
-
-    def filter_ends(field, slot, way):
-        filter_places(field, slot, way, [*range(outer), *range(groups - outer, groups)])
-
+            planes_and_rows(field, way, places[first : first + batch], put)
+
+    count = groups - 2 * outer
+    step = batch if count % batch == 0 else 1
+    turns = count // step
+
+    def filter_middle(field, way, put, begin, end):
+        if end > begin:
+
+            @pl.loop(begin, end)
+            def _(turn):
+                first = outer + turn * step
+                planes_and_rows(field, way, [first + k for k in range(step)], put)
+
+    def send_ends(slot, piece):
         @pl.when(line > 0)
         def _():
-            edge_copy(slot, False).start()
+            edge_copy(slot, False, piece).start()
 
         @pl.when(line < last)
         def _():
-            edge_copy(slot, True).start()
-
-    def filter_middle(field, slot, way):
-        count = groups - 2 * outer
-        step = batch if count % batch == 0 else 1
-        if inner:
-
-            @pl.loop(0, count // step)
-            def _(turn):
-                first = outer + turn * step
-                planes_and_rows(field, slot, way, [first + k for k in range(step)])
-
-    def wait_ends(slot):
+            edge_copy(slot, True, piece).start()
+
+    def wait_ends(slot, piece):
         @pl.when(line > 0)
         def _():
-            edge_copy(slot, False).wait_send()
-            edge_copy(slot, True).wait_recv()
+            edge_copy(slot, False, piece).wait_send()
+            edge_copy(slot, True, piece).wait_recv()
 
         @pl.when(line < last)
         def _():
-            edge_copy(slot, True).wait_send()
-            edge_copy(slot, False).wait_recv()
+            edge_copy(slot, True, piece).wait_send()
+            edge_copy(slot, False, piece).wait_recv()
 
     def out_copy(chunk, target_gy):
         part = pl.ds(chunk * (planes // CHUNKS), planes // CHUNKS)
@@ -394,72 +399,79 @@
 
     top = groups - outer
 
-    def middle_lines(slot, way, use):
+    def middle_lines(slot, use):
         if inner:
 
             @pl.loop(0, planes // 2, unroll=max(unroll // 2, 1))
             def _(turn):
-                for k, value in enumerate(along_middle(slot, way, 2 * turn)):
-                    use(2 * turn + k, value)
+                for k, value in enumerate(along_middle(slot, slot, 2 * turn)):
+                    use(2 * turn + k, outer, value)
+
+    def end_lines(slot, piece, use):
+        wait_ends(slot, piece)
+
+        @pl.loop(piece * per_piece, (piece + 1) * per_piece, unroll=min(unroll, per_piece))
+        def _(plane):
+            low, high = along_ends(slot, slot, plane)
+            use(plane, 0, low)
+            use(plane, top, high)
 
     def to_ratio(plane, first, value):
         known = lines(cleaned, plane, first, value.shape[0] // SUB)
-        keep(ratio, plane, first, known / (value + BACKGROUND))
-
-    filter_ends(cleaned, 0, 0)
+        keep(wide1, plane, outer + first, known / (value + BACKGROUND))
+
+    def to_blurred(plane, first, value):
+        keep(ratio, plane, first, value)
+
+    def to_wide(group, cell, value):
+        set_cell(wide0, outer + group, cell, value)
+
+    def forward_ends(source):
+        filter_ends(source, 0, to_wide)
+        for piece in range(PIECES):
+            send_ends(0, piece)
+
+    forward_ends(cleaned)
     for iteration in range(ITERS):
         source = cleaned if iteration == 0 else estimate
-
-        def to_estimate(plane, first, value):
-            keep(estimate, plane, first, lines(source, plane, first, value.shape[0] // SUB) * value)
-
-        filter_middle(source, 0, 0)
-        middle_lines(0, 0, lambda plane, value: to_ratio(plane, outer, value))
-        wait_ends(0)
-
-        @pl.loop(0, planes, unroll=unroll)
+        more = iteration < ITERS - 1
+        early = max(turns - 1, 0) if more else turns
+
+        def to_estimate(group, cell, value):
+            set_cell(estimate, group, cell, get_cell(source, group, cell) * value)
+
+        filter_middle(source, 0, to_wide, 0, turns)
+        middle_lines(0, to_ratio)
+        for piece in range(PIECES):
+            end_lines(0, piece, to_ratio)
+            send_ends(1, piece)
+        middle_lines(1, to_blurred)
+        filter_middle(ratio, 1, to_estimate, 0, early)
+        for piece in range(PIECES):
+            end_lines(1, piece, to_blurred)
+        filter_ends(ratio, 1, to_estimate)
+        if more:
+            forward_ends(estimate)
+        filter_middle(ratio, 1, to_estimate, early, turns)
+
+    for chunk in range(CHUNKS):
+
+        @pl.loop(chunk * (planes // CHUNKS), (chunk + 1) * (planes // CHUNKS), unroll=unroll)
         def _(plane):
-            low, high = along_ends(0, 0, plane)
-            to_ratio(plane, 0, low)
-            to_ratio(plane, top, high)
-
-        filter_ends(ratio, 1, 1)
-        filter_middle(ratio, 1, 1)
-        middle_lines(1, 1, lambda plane, value: to_estimate(plane, outer, value))
-        wait_ends(1)
-        if iteration < ITERS - 1:
-
-            @pl.loop(0, planes, unroll=unroll)
-            def _(plane):
-                low, high = along_ends(1, 1, plane)
-                to_estimate(plane, 0, low)
-                to_estimate(plane, top, high)
-
-            filter_ends(estimate, 0, 0)
-        else:
-            for chunk in range(CHUNKS):
-
-                @pl.loop(chunk * (planes // CHUNKS), (chunk + 1) * (planes // CHUNKS), unroll=unroll)
-                def _(plane):
-                    low, high = along_ends(1, 1, plane)
-                    pieces = [lines(source, plane, 0, outer) * low]
-                    if inner:
-                        pieces.append(lines(estimate, plane, outer, groups - 2 * outer))
-                    pieces.append(lines(source, plane, top, outer) * high)
-                    value = jnp.concatenate(pieces, axis=0).T
-                    for target in range(count_gy):
-                        stage[target, plane] = value[target * lines_x : (target + 1) * lines_x]
-
-                for step in range(count_gy):
-                    target = lax.rem(gy + 1 + step, count_gy)
-
-                    @pl.when(is_own(target))
-                    def _():
-                        own_copy(chunk).start()
-
-                    @pl.when(jnp.logical_not(is_own(target)))
-                    def _():
-                        out_copy(chunk, target).start()
+            value = lines(estimate, plane, 0, groups).T
+            for target in range(count_gy):
+                stage[target, plane] = value[target * lines_x : (target + 1) * lines_x]
+
+        for step_gy in range(count_gy):
+            target = lax.rem(gy + 1 + step_gy, count_gy)
+
+            @pl.when(is_own(target))
+            def _():
+                own_copy(chunk).start()
+
+            @pl.when(jnp.logical_not(is_own(target)))
+            def _():
+                out_copy(chunk, target).start()
 
     for chunk in range(CHUNKS):
         part = pl.ds(chunk * (planes // CHUNKS), planes // CHUNKS)
@@ -527,8 +539,8 @@
             pltpu.VMEM((2, 2 * max(cells - 2 * edge, edge), 2 * cells), jnp.bfloat16),
             pltpu.VMEM((2, 2 * edge, 6 * edge), jnp.bfloat16),
             pltpu.VMEM((lines_x, lines_y), jnp.float32),
-            pltpu.SemaphoreType.DMA((2, 2)),
-            pltpu.SemaphoreType.DMA((2, 2)),
+            pltpu.SemaphoreType.DMA((2, 2, PIECES)),
+            pltpu.SemaphoreType.DMA((2, 2, PIECES)),
             pltpu.SemaphoreType.DMA((CHUNKS, count_gy)),
             pltpu.SemaphoreType.DMA((CHUNKS, channels, per_gx)),
             pltpu.SemaphoreType.DMA((CHUNKS,)),

time: 106 us -> 101 us (0.953)
  Pallas kernels: 102 us -> 97.7 us
    pallas_call x1, Pallas kernels: 102 us -> 97.7 us  [local(): pl.pallas_call(functools.partial(deconvolve_kernel, count_gx, count_gy, e...]
where the time goes in v3:
time: 101 us
  Pallas kernels  97.7 us (97%)
  local copies, waits for them, and re-layouts  3.1 us (3%)
    pallas_call x1, Pallas kernels, local(): pl.pallas_call(functools.partial(deconvolve_kernel, count_gx, count_gy, e...  97.7 us
    reshape x1, local copies, waits for them, and re-layouts, local(): jnp.transpose(gathered, (0, 2, 3, 1, 4))  3.1 us

profile of v3, /device:TPU:1, one launch (start us, length us, event | category | flops | bytes accessed | tf_op | source)
XLA Modules:
  0.0 100.8 jit_solution(14784502940163403672)
XLA Ops:
  0.0 97.7 %shard_map.28 = f32[2,2,32,32,128]{4,3,2,1,0:T(8,128)} custom-call(f32[2,1,128,2048]{3,2,1,0:T(8,128)} %raw.1, f32[3,2,31]{2,1,0:T(2,128)} %taps.1), custom_call_target="tpu_custom_call" | custom-call | tf_op jit(solution)/shard_map/pallas_call | solution.py:521
  97.7 3.1 %copy_bitcast_fusion = f32[2,32,32,256]{3,2,1,0:T(8,128)} fusion(f32[2,2,32,32,128]{4,3,2,1,0:T(8,128)} %shard_map.28), kind=kLoop, calls=%fused_computation | loop fusion | bytes 4194304 | tf_op jit(solution)/shard_map/reshape | solution.py:555

commit v4 on v3

--- a/solution.py
+++ b/solution.py
@@ -14,6 +14,7 @@
 SUB = 8
 CHUNKS = 4
 PIECES = 4
+MOVES = 4
 MESH = pl.DeviceIdType.MESH
 
 
@@ -377,11 +378,16 @@
             edge_copy(slot, True, piece).wait_send()
             edge_copy(slot, False, piece).wait_recv()
 
+    def landing(channel, slot, part):
+        if cells % 128:
+            return out.at[channel, slot, part]
+        return out.at[channel, part, :, pl.ds(pl.multiple_of(slot * cells, cells), cells)]
+
     def out_copy(chunk, target_gy):
         part = pl.ds(chunk * (planes // CHUNKS), planes // CHUNKS)
         return pltpu.make_async_remote_copy(
             src_ref=stage.at[target_gy, part],
-            dst_ref=out.at[mine, place % per_gx, part],
+            dst_ref=landing(mine, place % per_gx, part),
             send_sem=out_send.at[chunk, target_gy],
             recv_sem=out_recv.at[chunk, mine, place % per_gx],
             device_id=(pair * 2 + place // per_gx, target_gy),
@@ -391,7 +397,7 @@
     def own_copy(chunk):
         part = pl.ds(chunk * (planes // CHUNKS), planes // CHUNKS)
         return pltpu.make_async_copy(
-            stage.at[gy, part], out.at[mine, place % per_gx, part], own_sem.at[chunk]
+            stage.at[gy, part], landing(mine, place % per_gx, part), own_sem.at[chunk]
         )
 
     def is_own(target_gy):
@@ -493,12 +499,34 @@
                 def _():
                     pltpu.make_async_remote_copy(
                         src_ref=stage.at[0, part],
-                        dst_ref=out.at[channel, slot, part],
+                        dst_ref=landing(channel, slot, part),
                         send_sem=out_send.at[chunk, 0],
                         recv_sem=out_recv.at[chunk, channel, slot],
                         device_id=(gx, gy),
                         device_id_type=MESH,
                     ).wait_recv()
+
+
+def hand_over(source, target, held, load_sem, store_sem):
+    channels, planes = source.shape[:2]
+    part = planes // MOVES
+    spots = [(channel, pl.ds(move * part, part)) for channel in range(channels) for move in range(MOVES)]
+
+    def load(index):
+        spot = spots[index]
+        return pltpu.make_async_copy(source.at[spot], held.at[spot], load_sem.at[index])
+
+    def store(index):
+        spot = spots[index]
+        return pltpu.make_async_copy(held.at[spot], target.at[spot], store_sem.at[index])
+
+    for index in range(len(spots)):
+        load(index).start()
+    for index in range(len(spots)):
+        load(index).wait()
+        store(index).start()
+    for index in range(len(spots)):
+        store(index).wait()
 
 
 def local(raw_stack, psf_taps):
@@ -518,9 +546,12 @@
     block_x = lines_x // count_gy
     field = pltpu.VMEM((groups, planes, SUB, lines_x), jnp.float32)
     wide = pltpu.VMEM((groups + 2 * outer, planes, SUB, lines_x), jnp.float32)
+    shape = (channels, planes, block_x, per_gx * cells)
+    if cells % 128:
+        shape = (channels, per_gx, planes, block_x, cells)
     gathered = pl.pallas_call(
         functools.partial(deconvolve_kernel, count_gx, count_gy, edge),
-        out_shape=jax.ShapeDtypeStruct((channels, per_gx, planes, block_x, cells), jnp.float32),
+        out_shape=jax.ShapeDtypeStruct(shape, jnp.float32),
         in_specs=[pl.BlockSpec(memory_space=pl.ANY), pl.BlockSpec(memory_space=pltpu.SMEM)],
         out_specs=pl.BlockSpec(memory_space=pl.ANY),
         scratch_shapes=[
@@ -552,9 +583,21 @@
             collective_id=0, has_side_effects=True, vmem_limit_bytes=67043328
         ),
     )(raw_stack, psf_taps)
-    return jnp.transpose(gathered, (0, 2, 3, 1, 4)).reshape(
-        channels, planes, block_x, per_gx * cells
-    )
+    if cells % 128:
+        gathered = jnp.transpose(gathered, (0, 2, 3, 1, 4))
+        return gathered.reshape(channels, planes, block_x, per_gx * cells)
+    return pl.pallas_call(
+        hand_over,
+        out_shape=jax.ShapeDtypeStruct(shape, jnp.float32),
+        in_specs=[pl.BlockSpec(memory_space=pl.ANY)],
+        out_specs=pl.BlockSpec(memory_space=pl.ANY),
+        scratch_shapes=[
+            pltpu.VMEM(shape, jnp.float32),
+            pltpu.SemaphoreType.DMA((channels * MOVES,)),
+            pltpu.SemaphoreType.DMA((channels * MOVES,)),
+        ],
+        compiler_params=pltpu.CompilerParams(vmem_limit_bytes=67043328),
+    )(gathered)
 
 
 def solution(mesh):

time: 101 us -> 101 us (level)
  local copies, waits for them, and re-layouts: 3.1 us -> 0 us
  Pallas kernels: 97.7 us -> 100 us
    reshape x1 -> x0, local copies, waits for them, and re-layouts: 3.1 us -> none  [local(): jnp.transpose(gathered, (0, 2, 3, 1, 4))]
    pallas_call x0 -> x1, Pallas kernels: none -> 2.39 us  [local(): pl.pallas_call(hand_over, out_shape=jax.ShapeDtypeStruct(shape, jnp.float...]
where the time goes in v4:
time: 101 us; the launch traced here: 100 us
  Pallas kernels  100 us (99%)
    pallas_call x1, Pallas kernels, local(): pl.pallas_call(functools.partial(deconvolve_kernel, count_gx, count_gy, e...  97.7 us
    pallas_call x1, Pallas kernels, local(): pl.pallas_call(hand_over, out_shape=jax.ShapeDtypeStruct(shape, jnp.float...  2.39 us

profile of v4, /device:TPU:1, one launch (start us, length us, event | category | flops | bytes accessed | tf_op | source)
XLA Modules:
  0.0 100.1 jit_solution(8363410608328295943)
XLA Ops:
  0.0 97.7 %shard_map.28.source = f32[2,32,32,256]{3,2,1,0:T(8,128)} custom-call(f32[2,1,128,2048]{3,2,1,0:T(8,128)} %raw.1, f32[3,2,31]{2,1,0:T(2,128)} %taps.1), custom_call_target="tpu_custom_call" | custom-call | tf_op jit(solution)/shard_map/pallas_call | solution.py:552
  97.7 2.4 %shard_map.29 = f32[2,32,32,256]{3,2,1,0:T(8,128)} custom-call(f32[2,32,32,256]{3,2,1,0:T(8,128)} %shard_map.28.source), custom_call_target="tpu_custom_call" | custom-call | tf_op jit(solution)/shard_map/pallas_call | solution.py:589

commit v5 on v4

--- a/solution.py
+++ b/solution.py
@@ -15,6 +15,7 @@
 CHUNKS = 4
 PIECES = 4
 MOVES = 4
+AHEAD = 1
 MESH = pl.DeviceIdType.MESH
 
 
@@ -121,6 +122,9 @@
     lines_x = width // count_gy
     me = gx * count_gy + gy
 
+    def block_at(step):
+        return lax.rem(step + (line + 1) // per_block + blocks // 2, blocks)
+
     def load(channel):
         return pltpu.make_async_copy(raw.at[channel, 0], held, held_sem)
 
@@ -130,8 +134,12 @@
     load(channel_of(0)).start()
     barrier = pltpu.get_barrier_semaphore()
 
+    low = 1 - pair * 2 // (count_gx // 2)
+
     @pl.loop(0, count_gx * count_gy)
-    def _(other):
+    def _(turn):
+        other = low * (count_gx * count_gy - 1 - turn) + (1 - low) * turn
+
         @pl.when(other != me)
         def _():
             pl.semaphore_signal(
@@ -212,15 +220,9 @@
         def _(index):
             smooth_block(index)
 
-        if turn == 0:
-            pl.semaphore_wait(barrier, count_gx * count_gy - 1)
-
-        @pl.loop(0, blocks)
-        def _(step):
-            index = lax.rem(step + (line + 1) // per_block + blocks // 2, blocks)
-            clean_block(channel, index)
+        def send_block(step):
             for part in range(per_block):
-                chunk = index * per_block + part
+                chunk = block_at(step) * per_block + part
 
                 @pl.when(is_own_plane(channel, chunk))
                 def _():
@@ -229,6 +231,25 @@
                 @pl.when(jnp.logical_not(is_own_plane(channel, chunk)))
                 def _():
                     plane_copy(channel, chunk).start()
+
+        ahead = 0
+        if turn == 0:
+            ahead = min(AHEAD, blocks)
+
+            @pl.loop(0, ahead)
+            def _(step):
+                clean_block(channel, block_at(step))
+
+            pl.semaphore_wait(barrier, count_gx * count_gy - 1)
+
+            @pl.loop(0, ahead)
+            def _(step):
+                send_block(step)
+
+        @pl.loop(ahead, blocks)
+        def _(step):
+            clean_block(channel, block_at(step))
+            send_block(step)
 
     fill_tables(taps, mine, edge, cells, depth, rows, middle, ends)
 
@@ -246,14 +267,6 @@
             wide[slot][outer + groups :] = zeros
 
     own_plane.wait()
-    for channel in range(channels):
-
-        @pl.loop(0, chunks)
-        def _(chunk):
-            @pl.when(jnp.logical_not(is_own_plane(channel, chunk)))
-            def _():
-                plane_copy(channel, chunk).wait_send()
-
     @pl.loop(0, count_gx * count_gy)
     def _(other):
         @pl.when(other != me)
@@ -478,6 +491,14 @@
             @pl.when(jnp.logical_not(is_own(target)))
             def _():
                 out_copy(chunk, target).start()
+
+    for channel in range(channels):
+
+        @pl.loop(0, chunks)
+        def _(chunk):
+            @pl.when(jnp.logical_not(is_own_plane(channel, chunk)))
+            def _():
+                plane_copy(channel, chunk).wait_send()
 
     for chunk in range(CHUNKS):
         part = pl.ds(chunk * (planes // CHUNKS), planes // CHUNKS)

time: 101 us -> 100 us (0.990)
  no operation moved by 1% of the time
where the time goes in v5:
time: 100 us; the launch traced here: 99.5 us
  Pallas kernels  99.5 us (100%)
    pallas_call x1, Pallas kernels, local(): pl.pallas_call(functools.partial(deconvolve_kernel, count_gx, count_gy, e...  97.1 us
    pallas_call x1, Pallas kernels, local(): pl.pallas_call(hand_over, out_shape=jax.ShapeDtypeStruct(shape, jnp.float...  2.39 us

profile of v5, /device:TPU:1, one launch (start us, length us, event | category | flops | bytes accessed | tf_op | source)
XLA Modules:
  0.0 99.5 jit_solution(11937202688351787806)
XLA Ops:
  0.0 97.1 %shard_map.28.source = f32[2,32,32,256]{3,2,1,0:T(8,128)} custom-call(f32[2,1,128,2048]{3,2,1,0:T(8,128)} %raw.1, f32[3,2,31]{2,1,0:T(2,128)} %taps.1), custom_call_target="tpu_custom_call" | custom-call | tf_op jit(solution)/shard_map/pallas_call | solution.py:573
  97.1 2.4 %shard_map.29 = f32[2,32,32,256]{3,2,1,0:T(8,128)} custom-call(f32[2,32,32,256]{3,2,1,0:T(8,128)} %shard_map.28.source), custom_call_target="tpu_custom_call" | custom-call | tf_op jit(solution)/shard_map/pallas_call | solution.py:610
